TPU v7x, 512 devices: a whole 4x8x8 slice. The times are simulated.
512 devices in a mesh: ang: 128 (over x, z, y_lo), rad: 4 (over y_hi, core).
Axes of the slice: x: 4, y: 8 (y_hi: 2, y_lo: 4; y = y_hi * 4 + y_lo), z: 8, core: 2. Of those that a mesh axis runs over, the one named last changes fastest.
Arguments:
- panel_slot: int32 [1048576], P(('ang', 'rad')), may hold values from 0 to 2047, as said below
- quad_points: float32 [9, 1048576], P(None, ('ang', 'rad')), may hold values from -27 to 27, as said below
- quad_weights: float32 [3, 1048576], P(None, ('ang', 'rad')), may hold values from 0.3 to 1
- densities: float32 [16, 1048576], P(None, ('ang', 'rad')), may hold values from -6 to 6
- near_pairs: int32 [128, 4, 4, 2, 4], P('ang', 'rad'), may hold values from 0 to 3, as said below
- quad_order: int32 [128, 4, 4, 4], P('ang', 'rad'), may hold values from 1 to 3, as said below
Outputs:
- potential: float32 [16, 1048576], P(None, ('ang', 'rad'))
Inputs may be any that keep to these rules, and one draw needn't show every extreme that they name: `panel_slot`: each group of 2048 consecutive panels holds every slot 0 to 2047 once. `quad_points`: row 3 k + c holds coordinate c of quadrature point k. `near_pairs`: for each sector, band and link the 4 pairs are distinct; on link 3 every source block is 0 and the target blocks are 0 to 3, each once. `quad_order`: each entry is 1 or 3.
All inputs are finite; a program needn't handle non-finite values.
Results may differ from a plain program's by a relative error of at most 0.0003.
Values sent between devices are 32-bit elements; how exact they have to be, the bound alone decides.
A program may use at most 64 MiB of HBM per device.

v0:
```python
import math

import jax
import jax.numpy as jnp
from jax import lax
from jax.experimental import pallas as pl
from jax.experimental.pallas import tpu as pltpu
from jax.sharding import PartitionSpec as P

NCOL = 16
PAN = 2048
BLK = 512
NBLK = PAN // BLK
ROWS = 32
DEPTH = 128
HALF = 256
MESH = pl.DeviceIdType.MESH
F32 = jnp.float32
BF16 = jnp.bfloat16

softening = 0.01
green_scale = 0.25 / math.pi

MINOR = (((1,), (1,)), ((), ()))


def split3(value):
    high = value.astype(BF16).astype(F32)
    rest = value - high
    middle = rest.astype(BF16).astype(F32)
    return high, middle, rest - middle


def dot(a, b):
    return jnp.dot(a, b, preferred_element_type=F32)


def dot_minor(a, b):
    return lax.dot_general(a, b, MINOR, preferred_element_type=F32)


def parts_of(raw_ref, variant, count):
    first, second, third = (raw_ref[pl.ds(16 + 3 * k, 3), :] for k in range(3))
    w = raw_ref[pl.ds(25, 3), :]
    area = w[0:1] + w[1:2] + w[2:3]
    if variant < 3:
        x = (first, second, third)[variant]
        weight = w[variant : variant + 1]
    else:
        x = (first + second + third) / 3.0
        weight = area / 3.0
    a = jnp.round(x * 8.0) * 0.125
    rest = x - a
    b = rest.astype(BF16).astype(F32)
    c = (rest - b).astype(BF16).astype(F32)
    fine = b + c
    square = jnp.sum(a * a, axis=0, keepdims=True)
    linear = jnp.sum(2.0 * a * fine + fine * fine, axis=0, keepdims=True) + softening * area
    return a, b, c, split3(square), split3(linear), weight


def stage_source(stage, raw_ref, variant, count):
    a, b, c, square, linear, weight = parts_of(raw_ref, variant, count)
    cols = slice(0, count)
    stage[0:3, cols] = -2.0 * a
    ones = jnp.ones((3, count), F32)
    for row, values in ((8, square), (16, linear)):
        stage[row : row + 3, cols] = ones
        for index in range(3):
            stage[row + 3 + index : row + 4 + index, cols] = values[index]
    for row, value in ((24, b), (32, c), (40, a), (48, a), (56, b), (64, c), (72, b), (80, c)):
        stage[row : row + 3, cols] = -2.0 * value
    return weight


def stage_target(stage, raw_ref, variant, count):
    a, b, c, square, linear, weight = parts_of(raw_ref, variant, count)
    stage[0:3, :] = a
    ones = jnp.ones((3, count), F32)
    for row, values in ((8, square), (16, linear)):
        stage[row + 3 : row + 6, :] = ones
        for index in range(3):
            stage[row + index : row + 1 + index, :] = values[index]
    for row, value in ((24, a), (32, a), (40, b), (48, c), (56, b), (64, b), (72, c), (80, c)):
        stage[row : row + 3, :] = value
    for index, value in enumerate(split3(weight * green_scale)):
        stage[88 + index : 89 + index, :] = value


def kernel(
    sectors,
    bands,
    pair_ref,
    order_ref,
    slot_ref,
    points_ref,
    weights_ref,
    densities_ref,
    out_ref,
    onehot,
    raw,
    near1,
    near2,
    edge,
    stage,
    target,
    target_weight,
    source,
    source_weight,
    density,
    tile_high,
    tile_low,
    result,
    sent1,
    sent2,
    sent3,
    back1,
    back2,
    back3,
    send_sem,
    recv_sem,
):
    sector = lax.axis_index("ang")
    band = lax.axis_index("rad")

    def at_sector(step):
        return (lax.rem(sector + step + sectors, sectors), band)

    inner = (sector, jnp.maximum(band - 1, 0))
    outer = (sector, jnp.minimum(band + 1, bands - 1))
    has_inner = band > 0
    has_outer = band < bands - 1

    def remote(src, dst, index, device):
        return pltpu.make_async_remote_copy(
            src_ref=src,
            dst_ref=dst,
            send_sem=send_sem.at[index],
            recv_sem=recv_sem.at[index],
            device_id=device,
            device_id_type=MESH,
        )

    out1 = remote(raw, near1, 0, at_sector(-1))
    out2 = remote(raw, near2, 1, at_sector(-2))
    out3 = remote(raw.at[:, pl.ds(0, BLK)], edge, 2, inner)
    ret1 = remote(sent1, back1, 3, at_sector(1))
    ret2 = remote(sent2, back2, 4, at_sector(2))
    ret3 = remote(sent3, back3, 5, outer)

    barrier = pltpu.get_barrier_semaphore()
    for step in (-2, -1, 1, 2):
        pl.semaphore_signal(barrier, inc=1, device_id=at_sector(step), device_id_type=MESH)

    @pl.when(has_inner)
    def _():
        pl.semaphore_signal(barrier, inc=1, device_id=inner, device_id_type=MESH)

    @pl.when(has_outer)
    def _():
        pl.semaphore_signal(barrier, inc=1, device_id=outer, device_id_type=MESH)

    slots = slot_ref[...]
    values = jnp.concatenate(
        [densities_ref[...], points_ref[...], weights_ref[...], jnp.zeros((4, PAN), F32)], axis=0
    )
    pieces = jnp.concatenate([piece.astype(BF16) for piece in split3(values)], axis=0)

    def permute(block, carry):
        rows = pl.ds(pl.multiple_of(block * HALF, HALF), HALF)
        index = lax.broadcasted_iota(jnp.int32, (HALF, PAN), 0) + block * HALF
        hot = jnp.where(index == slots, 1.0, 0.0).astype(BF16)
        onehot[rows, :] = hot
        moved = dot_minor(pieces, hot)
        raw[:, rows] = moved[0:32] + moved[32:64] + moved[64:96]
        return carry

    lax.fori_loop(0, PAN // HALF, permute, 0)

    pl.semaphore_wait(barrier, 4 + jnp.minimum(band, 1) + jnp.minimum(bands - 1 - band, 1))

    @pl.when(has_inner)
    def _():
        out3.start()

    out2.start()
    out1.start()

    stage[...] = jnp.zeros_like(stage)
    pick = jnp.where(
        jnp.logical_and(
            lax.broadcasted_iota(jnp.int32, (DEPTH, 128), 0) >= 88,
            lax.broadcasted_iota(jnp.int32, (DEPTH, 128), 0) < 91,
        ),
        1.0,
        0.0,
    ).astype(BF16)
    for variant in range(4):
        stage_target(stage, raw, variant, PAN)
        for index in range(NBLK):
            turned = stage[:, index * BLK : (index + 1) * BLK].T.astype(BF16)
            target[4 * index + variant] = turned
            target_weight[4 * index + variant] = dot(turned, pick)
    stage[...] = jnp.zeros_like(stage)

    def load_source(link, raw_ref, count):
        for variant in range(4):
            weight = stage_source(stage, raw_ref, variant, count)
            for index in range(count // HALF):
                cols = slice(index * HALF, (index + 1) * HALF)
                place = ((link * NBLK + index // 2) * 4 + variant) * 2 + index % 2
                source[place] = stage[:, cols].astype(BF16)
                source_weight[place] = weight[:, cols]
        for index in range(count // BLK):
            d = raw_ref[0:16, index * BLK : (index + 1) * BLK]
            high = d.astype(BF16)
            density[link * NBLK + index, 0:16, :] = high
            density[link * NBLK + index, 16:32, :] = (d - high.astype(F32)).astype(BF16)

    load_source(0, raw, PAN)
    result[...] = jnp.zeros_like(result)
    sent1[...] = jnp.zeros_like(sent1)
    sent2[...] = jnp.zeros_like(sent2)
    sent3[...] = jnp.zeros_like(sent3)

    def tile(step, carry):
        link = lax.rem(3 * lax.div(step + 3, 4), 4)
        entry = lax.rem(step + 3, 4)

        @pl.when(jnp.logical_and(step == 1, has_outer))
        def _():
            out3.wait_recv()
            load_source(3, edge, BLK)

        @pl.when(step == 5)
        def _():
            @pl.when(has_outer)
            def _():
                ret3.start()

            out2.wait_recv()
            load_source(2, near2, PAN)

        @pl.when(step == 9)
        def _():
            ret2.start()
            out1.wait_recv()
            load_source(1, near1, PAN)

        @pl.when(step == 13)
        def _():
            ret1.start()

        @pl.when(jnp.logical_or(link != 3, has_outer))
        def _():
            target_block = pair_ref[link * 8 + entry]
            source_block = pair_ref[link * 8 + 4 + entry]
            order = order_ref[link * 4 + entry]
            variants = [jnp.where(order == 3, k, 3) for k in range(3)]
            source_place = link * NBLK + source_block
            for half in range(BLK // HALF):
                block = None
                for k in range(3):
                    points = target[4 * target_block + variants[k]]
                    inner_sum = None
                    for l in range(3):
                        place = (4 * source_place + variants[l]) * 2 + half
                        term = lax.rsqrt(dot(points, source[place])) * source_weight[place]
                        inner_sum = term if inner_sum is None else inner_sum + term
                    scale = target_weight[4 * target_block + variants[k]]
                    term = inner_sum * jnp.concatenate([scale, scale], axis=1)
                    block = term if block is None else block + term
                high = block.astype(BF16)
                tile_high[:, half * HALF : (half + 1) * HALF] = high
                tile_low[:, half * HALF : (half + 1) * HALF] = (block - high.astype(F32)).astype(BF16)
            high = tile_high[...]
            low = tile_low[...]
            far = density[source_place]
            full = dot_minor(far, high)
            forward = full[0:16] + full[16:32] + dot_minor(far[0:16], low)
            for index in range(NBLK):
                result[index] = result[index] + jnp.where(target_block == index, forward, 0.0)

            @pl.when(link != 0)
            def _():
                own = density[target_block]
                full = dot(own, high)
                backward = full[0:16] + full[16:32] + dot(own[0:16], low)

                @pl.when(link == 1)
                def _():
                    for index in range(NBLK):
                        sent1[index] = sent1[index] + jnp.where(source_block == index, backward, 0.0)

                @pl.when(link == 2)
                def _():
                    for index in range(NBLK):
                        sent2[index] = sent2[index] + jnp.where(source_block == index, backward, 0.0)

                @pl.when(link == 3)
                def _():
                    sent3[...] = sent3[...] + backward

        return carry

    lax.fori_loop(0, 16, tile, 0)

    @pl.when(has_inner)
    def _():
        ret3.wait_recv()
        result[0] = result[0] + back3[...]

    ret1.wait_recv()
    ret2.wait_recv()
    total = jnp.zeros((3 * NCOL, PAN), F32)
    for index in range(NBLK):
        block = result[index] + back1[index] + back2[index]
        moved = jnp.concatenate([piece.astype(BF16) for piece in split3(block)], axis=0)
        total = total + dot(moved, onehot[index * BLK : (index + 1) * BLK, :])
    out_ref[...] = total[0:16] + total[16:32] + total[32:48]

    out1.wait_send()
    out2.wait_send()
    ret1.wait_send()
    ret2.wait_send()

    @pl.when(has_inner)
    def _():
        out3.wait_send()

    @pl.when(has_outer)
    def _():
        ret3.wait_send()


def solution(mesh):
    sectors, bands = mesh.shape["ang"], mesh.shape["rad"]

    def on_device(panel_slot, quad_points, quad_weights, densities, near_pairs, quad_order):
        vmem = pl.BlockSpec(memory_space=pltpu.VMEM)
        smem = pl.BlockSpec(memory_space=pltpu.SMEM)

        def body(*refs):
            kernel(sectors, bands, *refs)

        return pl.pallas_call(
            body,
            name="near_field",
            out_shape=jax.ShapeDtypeStruct((NCOL, PAN), F32),
            in_specs=[smem, smem, vmem, vmem, vmem, vmem],
            out_specs=vmem,
            scratch_shapes=[
                pltpu.VMEM((PAN, PAN), BF16),
                pltpu.VMEM((ROWS, PAN), F32),
                pltpu.VMEM((ROWS, PAN), F32),
                pltpu.VMEM((ROWS, PAN), F32),
                pltpu.VMEM((ROWS, BLK), F32),
                pltpu.VMEM((DEPTH, PAN), F32),
                pltpu.VMEM((NBLK * 4, BLK, DEPTH), BF16),
                pltpu.VMEM((NBLK * 4, BLK, 128), F32),
                pltpu.VMEM((4 * NBLK * 8, DEPTH, HALF), BF16),
                pltpu.VMEM((4 * NBLK * 8, 1, HALF), F32),
                pltpu.VMEM((4 * NBLK, 2 * NCOL, BLK), BF16),
                pltpu.VMEM((BLK, BLK), BF16),
                pltpu.VMEM((BLK, BLK), BF16),
                pltpu.VMEM((NBLK, NCOL, BLK), F32),
                pltpu.VMEM((NBLK, NCOL, BLK), F32),
                pltpu.VMEM((NBLK, NCOL, BLK), F32),
                pltpu.VMEM((NCOL, BLK), F32),
                pltpu.VMEM((NBLK, NCOL, BLK), F32),
                pltpu.VMEM((NBLK, NCOL, BLK), F32),
                pltpu.VMEM((NCOL, BLK), F32),
                pltpu.SemaphoreType.DMA((6,)),
                pltpu.SemaphoreType.DMA((6,)),
            ],
            compiler_params=pltpu.CompilerParams(
                collective_id=0, has_side_effects=True, vmem_limit_bytes=60 * 1024 * 1024
            ),
        )(
            near_pairs.reshape(-1),
            quad_order.reshape(-1),
            panel_slot.reshape(1, PAN),
            quad_points,
            quad_weights,
            densities,
        )

    return jax.shard_map(
        on_device,
        mesh=mesh,
        in_specs=(
            P(("ang", "rad")),
            P(None, ("ang", "rad")),
            P(None, ("ang", "rad")),
            P(None, ("ang", "rad")),
            P("ang", "rad", None, None, None),
            P("ang", "rad", None, None),
        ),
        out_specs=P(None, ("ang", "rad")),
        check_vma=False,
    )
```

profile of v0, /device:TPU:32, one launch (start us, length us, event | category | flops | bytes accessed | tf_op | source)
XLA Modules:
  0.0 68.1 jit_solution(14255673148126017380)
XLA Ops:
  0.0 0.0 copy-start
  0.0 1.3 %reshape.9.refs_0_ = s32[32]{0:T(128)} reshape(s32[1,1,4,2,4]{4,3,2,1,0:T(2,128)} %param.10) | data formatting | bytes 256 | tf_op jit(solution)/shard_map/reshape | solution.py:380
  1.3 0.0 copy-done
  1.3 0.7 reshape.10.refs_1_
  2.0 64.5 %near_field.1 = f32[16,2048]{1,0:T(8,128)} custom-call(s32[32]{0:T(128)} %reshape.9.refs_0_, s32[16]{0:T(128)} %reshape.10.refs_1_, s32[1,2048]{1,0:T(1,128)} %bitcast.1, f32[9,2048]{1,0:T(8,128)} %refs_3_.1, f32[3,2048]{1,0:T(4,128)} %refs_4_.1, f32[16,2048]{1,0:T(8,128)} %refs_5_.1), custom_call_target="tpu_custom_call" | custom-call | tf_op jit(solution)/shard_map/near_field/pallas_call | solution.py:346
  66.5 1.6 %copy.8 = f32[16,2048]{1,0:T(8,128)} copy(f32[16,2048]{1,0:T(8,128)} %near_field.1) | data formatting | bytes 262144
Async XLA Ops:
  0.0 1.3 %copy-start = (s32[1,1,4,4]{3,2,1,0:T(4,128)S(1)}, s32[1,1,4,4]{3,2,1,0:T(4,128)}, u32[]{:S(2)}) copy-start(s32[1,1,4,4]{3,2,1,0:T(4,128)} %param.11) | copy-start | bytes 196
where the time goes:
time: 68.3 us; the launch traced here: 68.1 us
  Pallas kernels  64.5 us (94%)
  local copies, waits for them, and re-layouts  3.53 us (5%)
    pallas_call x1, Pallas kernels, on_device(): pl.pallas_call(body, name='near_field', out_shape=jax.ShapeDtypeStruct((N...  64.5 us
    unnamed x3, local copies, waits for them, and re-layouts  1.57 us

commit v1 on v0

--- a/solution.py
+++ b/solution.py
@@ -11,7 +11,7 @@
 PAN = 2048
 BLK = 512
 NBLK = PAN // BLK
-ROWS = 32
+ROWS = 28
 DEPTH = 128
 HALF = 256
 MESH = pl.DeviceIdType.MESH
@@ -97,7 +97,6 @@
     weights_ref,
     densities_ref,
     out_ref,
-    onehot,
     raw,
     near1,
     near2,
@@ -142,7 +141,7 @@
         )
 
     out1 = remote(raw, near1, 0, at_sector(-1))
-    out2 = remote(raw, near2, 1, at_sector(-2))
+    relay = remote(near1, near2, 1, at_sector(-1))
     out3 = remote(raw.at[:, pl.ds(0, BLK)], edge, 2, inner)
     ret1 = remote(sent1, back1, 3, at_sector(1))
     ret2 = remote(sent2, back2, 4, at_sector(2))
@@ -162,7 +161,7 @@
 
     slots = slot_ref[...]
     values = jnp.concatenate(
-        [densities_ref[...], points_ref[...], weights_ref[...], jnp.zeros((4, PAN), F32)], axis=0
+        [densities_ref[...], points_ref[...], weights_ref[...], jnp.zeros((32 - ROWS, PAN), F32)], axis=0
     )
     pieces = jnp.concatenate([piece.astype(BF16) for piece in split3(values)], axis=0)
 
@@ -170,21 +169,11 @@
         rows = pl.ds(pl.multiple_of(block * HALF, HALF), HALF)
         index = lax.broadcasted_iota(jnp.int32, (HALF, PAN), 0) + block * HALF
         hot = jnp.where(index == slots, 1.0, 0.0).astype(BF16)
-        onehot[rows, :] = hot
         moved = dot_minor(pieces, hot)
-        raw[:, rows] = moved[0:32] + moved[32:64] + moved[64:96]
+        raw[:, rows] = (moved[0:32] + moved[32:64] + moved[64:96])[0:ROWS]
         return carry
 
     lax.fori_loop(0, PAN // HALF, permute, 0)
-
-    pl.semaphore_wait(barrier, 4 + jnp.minimum(band, 1) + jnp.minimum(bands - 1 - band, 1))
-
-    @pl.when(has_inner)
-    def _():
-        out3.start()
-
-    out2.start()
-    out1.start()
 
     stage[...] = jnp.zeros_like(stage)
     pick = jnp.where(
@@ -201,6 +190,15 @@
             turned = stage[:, index * BLK : (index + 1) * BLK].T.astype(BF16)
             target[4 * index + variant] = turned
             target_weight[4 * index + variant] = dot(turned, pick)
+    pl.semaphore_wait(barrier, 4 + jnp.minimum(band, 1) + jnp.minimum(bands - 1 - band, 1))
+
+    out1.start()
+
+    @pl.when(has_inner)
+    def _():
+        out3.start()
+
+
     stage[...] = jnp.zeros_like(stage)
 
     def load_source(link, raw_ref, count):
@@ -224,38 +222,39 @@
     sent3[...] = jnp.zeros_like(sent3)
 
     def tile(step, carry):
-        link = lax.rem(3 * lax.div(step + 3, 4), 4)
-        entry = lax.rem(step + 3, 4)
-
-        @pl.when(jnp.logical_and(step == 1, has_outer))
+        link = lax.rem(lax.div(step + 2, 4), 4)
+        entry = lax.rem(step + 2, 4)
+
+        @pl.when(step == 2)
         def _():
-            out3.wait_recv()
-            load_source(3, edge, BLK)
-
-        @pl.when(step == 5)
+            out1.wait_recv()
+            relay.start()
+            load_source(1, near1, PAN)
+
+        @pl.when(step == 6)
         def _():
+            ret1.start()
+            relay.wait_recv()
+            load_source(2, near2, PAN)
+
+        @pl.when(step == 10)
+        def _():
+            ret2.start()
+
             @pl.when(has_outer)
             def _():
-                ret3.start()
-
-            out2.wait_recv()
-            load_source(2, near2, PAN)
-
-        @pl.when(step == 9)
+                out3.wait_recv()
+                load_source(3, edge, BLK)
+
+        @pl.when(jnp.logical_and(step == 14, has_outer))
         def _():
-            ret2.start()
-            out1.wait_recv()
-            load_source(1, near1, PAN)
-
-        @pl.when(step == 13)
-        def _():
-            ret1.start()
+            ret3.start()
 
         @pl.when(jnp.logical_or(link != 3, has_outer))
         def _():
-            target_block = pair_ref[link * 8 + entry]
-            source_block = pair_ref[link * 8 + 4 + entry]
-            order = order_ref[link * 4 + entry]
+            target_block = pair_ref[0, 0, link, 0, entry]
+            source_block = pair_ref[0, 0, link, 1, entry]
+            order = order_ref[0, 0, link, entry]
             variants = [jnp.where(order == 3, k, 3) for k in range(3)]
             source_place = link * NBLK + source_block
             for half in range(BLK // HALF):
@@ -312,15 +311,11 @@
 
     ret1.wait_recv()
     ret2.wait_recv()
-    total = jnp.zeros((3 * NCOL, PAN), F32)
     for index in range(NBLK):
-        block = result[index] + back1[index] + back2[index]
-        moved = jnp.concatenate([piece.astype(BF16) for piece in split3(block)], axis=0)
-        total = total + dot(moved, onehot[index * BLK : (index + 1) * BLK, :])
-    out_ref[...] = total[0:16] + total[16:32] + total[32:48]
+        out_ref[:, index * BLK : (index + 1) * BLK] = result[index] + back1[index] + back2[index]
 
     out1.wait_send()
-    out2.wait_send()
+    relay.wait_send()
     ret1.wait_send()
     ret2.wait_send()
 
@@ -331,6 +326,20 @@
     @pl.when(has_outer)
     def _():
         ret3.wait_send()
+
+
+def restore(slot_ref, value_ref, out_ref):
+    lanes = 128
+    for first in range(0, PAN, lanes):
+        slots = jnp.broadcast_to(slot_ref[:, first : first + lanes], (NCOL, lanes))
+        lane = jnp.bitwise_and(slots, lanes - 1)
+        group = jnp.right_shift(slots, 7)
+        total = jnp.zeros((NCOL, lanes), F32)
+        for index in range(PAN // lanes):
+            part = value_ref[:, index * lanes : (index + 1) * lanes]
+            found = jnp.take_along_axis(part, lane, axis=1, mode="promise_in_bounds")
+            total = jnp.where(group == index, found, total)
+        out_ref[:, first : first + lanes] = total
 
 
 def solution(mesh):
@@ -343,14 +352,14 @@
         def body(*refs):
             kernel(sectors, bands, *refs)
 
-        return pl.pallas_call(
+        slots = panel_slot.reshape(1, PAN)
+        ordered = pl.pallas_call(
             body,
             name="near_field",
             out_shape=jax.ShapeDtypeStruct((NCOL, PAN), F32),
             in_specs=[smem, smem, vmem, vmem, vmem, vmem],
             out_specs=vmem,
             scratch_shapes=[
-                pltpu.VMEM((PAN, PAN), BF16),
                 pltpu.VMEM((ROWS, PAN), F32),
                 pltpu.VMEM((ROWS, PAN), F32),
                 pltpu.VMEM((ROWS, PAN), F32),
@@ -377,13 +386,20 @@
                 collective_id=0, has_side_effects=True, vmem_limit_bytes=60 * 1024 * 1024
             ),
         )(
-            near_pairs.reshape(-1),
-            quad_order.reshape(-1),
-            panel_slot.reshape(1, PAN),
+            near_pairs,
+            quad_order,
+            slots,
             quad_points,
             quad_weights,
             densities,
         )
+        return pl.pallas_call(
+            restore,
+            name="restore",
+            out_shape=jax.ShapeDtypeStruct((NCOL, PAN), F32),
+            in_specs=[vmem, vmem],
+            out_specs=vmem,
+        )(slots, ordered)
 
     return jax.shard_map(
         on_device,

time: 68.3 us -> 55.5 us (0.81)
  the two profiles are of different devices: /device:TPU:32 before, /device:TPU:1 now
where the time goes in v1:
time: 55.5 us; the launch traced here: 55.4 us
  Pallas kernels  55.4 us (100%)
    pallas_call x1, Pallas kernels, on_device(): pl.pallas_call(body, name='near_field', out_shape=jax.ShapeDtypeStruct((N...  53.1 us
    pallas_call x1, Pallas kernels, on_device(): pl.pallas_call(restore, name='restore', out_shape=jax.ShapeDtypeStruct((N...  2.23 us

profile of v1, /device:TPU:1, one launch (start us, length us, event | category | flops | bytes accessed | tf_op | source)
XLA Modules:
  0.0 55.4 jit_solution(1065454919017765909)
XLA Ops:
  0.0 53.1 %near_field.1.value_ref = f32[16,2048]{1,0:T(8,128)} custom-call(s32[1,1,4,2,4]{4,3,2,1,0:T(2,128)} %refs_0_.1, s32[1,1,4,4]{3,2,1,0:T(4,128)} %refs_1_.1, s32[1,2048]{1,0:T(1,128)} %bitcast.1, f32[9,2048]{1,0:T(8,128)} %refs_3_.1, f32[3,2048]{1,0:T(4,128)} %refs_4_.1, f32[16,2048]{1,0:T(8,128)} %refs_5_.1), custom_call_target="tpu_custom_call" | custom-call | tf_op jit(solution)/shard_map/near_field/pallas_call | solution.py:356
  53.2 2.2 %restore.1 = f32[16,2048]{1,0:T(8,128)} custom-call(s32[1,2048]{1,0:T(1,128)} %bitcast.2, f32[16,2048]{1,0:T(8,128)} %near_field.1.value_ref), custom_call_target="tpu_custom_call" | custom-call | tf_op jit(solution)/shard_map/restore/pallas_call | solution.py:396

commit v2 on v1

--- a/solution.py
+++ b/solution.py
@@ -148,7 +148,7 @@
     ret3 = remote(sent3, back3, 5, outer)
 
     barrier = pltpu.get_barrier_semaphore()
-    for step in (-2, -1, 1, 2):
+    for step in (-2, -1, 1):
         pl.semaphore_signal(barrier, inc=1, device_id=at_sector(step), device_id_type=MESH)
 
     @pl.when(has_inner)
@@ -173,7 +173,7 @@
         raw[:, rows] = (moved[0:32] + moved[32:64] + moved[64:96])[0:ROWS]
         return carry
 
-    lax.fori_loop(0, PAN // HALF, permute, 0)
+    lax.fori_loop(0, PAN // HALF, permute, 0, unroll=True)
 
     stage[...] = jnp.zeros_like(stage)
     pick = jnp.where(
@@ -190,14 +190,19 @@
             turned = stage[:, index * BLK : (index + 1) * BLK].T.astype(BF16)
             target[4 * index + variant] = turned
             target_weight[4 * index + variant] = dot(turned, pick)
-    pl.semaphore_wait(barrier, 4 + jnp.minimum(band, 1) + jnp.minimum(bands - 1 - band, 1))
-
-    out1.start()
-
-    @pl.when(has_inner)
-    def _():
-        out3.start()
-
+    def send_own():
+        pl.semaphore_wait(barrier, 3 + jnp.minimum(band, 1) + jnp.minimum(bands - 1 - band, 1))
+        out1.start()
+
+        @pl.when(has_inner)
+        def _():
+            out3.start()
+
+    patient = lax.rem(sector, 32) == 0
+
+    @pl.when(jnp.logical_not(patient))
+    def _():
+        send_own()
 
     stage[...] = jnp.zeros_like(stage)
 
@@ -222,22 +227,26 @@
     sent3[...] = jnp.zeros_like(sent3)
 
     def tile(step, carry):
-        link = lax.rem(lax.div(step + 2, 4), 4)
-        entry = lax.rem(step + 2, 4)
-
-        @pl.when(step == 2)
-        def _():
+        link = lax.rem(lax.div(step + 1, 4), 4)
+        entry = lax.rem(step + 1, 4)
+
+        @pl.when(step == 3)
+        def _():
+            @pl.when(patient)
+            def _():
+                send_own()
+
             out1.wait_recv()
             relay.start()
             load_source(1, near1, PAN)
 
-        @pl.when(step == 6)
+        @pl.when(step == 7)
         def _():
             ret1.start()
             relay.wait_recv()
             load_source(2, near2, PAN)
 
-        @pl.when(step == 10)
+        @pl.when(step == 11)
         def _():
             ret2.start()
 
@@ -246,7 +255,7 @@
                 out3.wait_recv()
                 load_source(3, edge, BLK)
 
-        @pl.when(jnp.logical_and(step == 14, has_outer))
+        @pl.when(jnp.logical_and(step == 15, has_outer))
         def _():
             ret3.start()
 

time: 55.5 us -> 55.6 us (level)
  the two profiles are of different devices: /device:TPU:1 before, /device:TPU:8 now
where the time goes in v2:
time: 55.6 us; the launch traced here: 55.4 us
  Pallas kernels  55.4 us (100%)
    pallas_call x1, Pallas kernels, on_device(): pl.pallas_call(body, name='near_field', out_shape=jax.ShapeDtypeStruct((N...  53.2 us
    pallas_call x1, Pallas kernels, on_device(): pl.pallas_call(restore, name='restore', out_shape=jax.ShapeDtypeStruct((N...  2.23 us

profile of v2, /device:TPU:8, one launch (start us, length us, event | category | flops | bytes accessed | tf_op | source)
XLA Modules:
  0.0 55.4 jit_solution(13107139679809107201)
XLA Ops:
  0.0 53.2 %near_field.1.value_ref = f32[16,2048]{1,0:T(8,128)} custom-call(s32[1,1,4,2,4]{4,3,2,1,0:T(2,128)} %refs_0_.1, s32[1,1,4,4]{3,2,1,0:T(4,128)} %refs_1_.1, s32[1,2048]{1,0:T(1,128)} %bitcast.1, f32[9,2048]{1,0:T(8,128)} %refs_3_.1, f32[3,2048]{1,0:T(4,128)} %refs_4_.1, f32[16,2048]{1,0:T(8,128)} %refs_5_.1), custom_call_target="tpu_custom_call" | custom-call | tf_op jit(solution)/shard_map/near_field/pallas_call | solution.py:365
  53.2 2.2 %restore.1 = f32[16,2048]{1,0:T(8,128)} custom-call(s32[1,2048]{1,0:T(1,128)} %bitcast.2, f32[16,2048]{1,0:T(8,128)} %near_field.1.value_ref), custom_call_target="tpu_custom_call" | custom-call | tf_op jit(solution)/shard_map/restore/pallas_call | solution.py:405
